TPU v7x, 32 devices: a whole 2x2x4 slice. The times are simulated.
32 devices in a mesh: groups: 2 (over x), space: 16 (over z, y, core).
Axes of the slice: x: 2, y: 2, z: 4, core: 2. Of those that a mesh axis runs over, the one named last changes fastest.
Arguments:
- eigvecs: bfloat16 [32, 64, 2, 3, 128], P('groups', 'space'), parts along dimension 0, may hold values from -1.3515625 to 1.3515625
- phase_index: int32 [128], P('groups'), parts along dimension 0, may hold values from 0 to 47
- perambulator: bfloat16 [512, 2, 128, 128], P(('groups', 'space')), parts along dimension 0, may hold values from -0.046875 to 0.046875
- tile_sink: int32 [512, 1], P(('groups', 'space')), parts along dimension 0, may hold values from 0 to 15; in each aligned block of 16 rows (0 to 15, 16 to 31, ...) at most 2 rows name the same one
- tile_sep: int32 [512], P(('groups', 'space')), parts along dimension 0, may hold values from 0 to 7
- tile_diagram: int32 [512], P(('groups', 'space')), parts along dimension 0, may hold values from 0 to 1
Outputs:
- elementals: bfloat16 [32, 2, 128, 128], P(('groups', 'space')), parts along dimension 0
- correlator: float32 [512, 2], P(('groups', 'space')), parts along dimension 0
There are 2 independent parts, one for each index of `groups`. A program takes and returns all parts, laid end to end along the dimension named above; each array names one. Nothing has to cross between parts.
Inputs may be any that keep to these rules, and one draw needn't show every extreme that they name: `tile_sink`: in the tiles of one device no sink time is named by more than 2 tiles.
All inputs are finite; a program needn't handle non-finite values.
Results may differ from a plain program's by a relative error of at most 0.0048.
Values may be sent and summed in bfloat16 or wider, within the bound.
A program may use at most 128 MiB of HBM per device.

v0:
```python
import math
import jax
import jax.numpy as jnp
from jax import lax
from jax.sharding import PartitionSpec as P

PERIOD = 48


def make_right(vecs, cosine, sine):
    real_part = vecs[..., 0, :, :].astype(jnp.float32)
    imag_part = vecs[..., 1, :, :].astype(jnp.float32)
    cos_col = cosine[:, None, None]
    sin_col = sine[:, None, None]
    first = (cos_col * real_part - sin_col * imag_part).astype(jnp.bfloat16)
    second = (sin_col * real_part + cos_col * imag_part).astype(jnp.bfloat16)
    top = jnp.stack([first, second], -2)
    bottom = jnp.stack([second, -first], -2)
    return jnp.stack([top, bottom], -4)


def phases(indices):
    angle = 2.0 * math.pi / PERIOD * indices.astype(jnp.float32)
    return (jnp.cos(angle), jnp.sin(angle))


def contract_tiles(sink_mat, source_mat, tiles, diagram):

    def mult(left, right):
        return jnp.einsum("bij,bjk->bik", left, right, preferred_element_type=jnp.float32)

    tile_re = tiles[:, 0]
    tile_im = tiles[:, 1]
    trans_re = jnp.swapaxes(tile_re, 1, 2)
    trans_im = -jnp.swapaxes(tile_im, 1, 2)
    flag = (diagram == 1)[:, None, None]
    left_re = jnp.where(flag, trans_re, tile_re)
    left_im = jnp.where(flag, trans_im, tile_im)
    right_re = jnp.where(flag, tile_re, trans_re)
    right_im = jnp.where(flag, tile_im, trans_im)
    sink_re = sink_mat[:, 0]
    sink_im = sink_mat[:, 1]
    src_re = jnp.swapaxes(source_mat[:, 0], 1, 2)
    src_im = -jnp.swapaxes(source_mat[:, 1], 1, 2)
    first_re = mult(sink_re, left_re) - mult(sink_im, left_im)
    first_im = mult(sink_re, left_im) + mult(sink_im, left_re)
    second_re = jnp.swapaxes(mult(src_re, right_re) - mult(src_im, right_im), 1, 2)
    second_im = jnp.swapaxes(mult(src_re, right_im) + mult(src_im, right_re), 1, 2)
    trace_re = jnp.sum(first_re * second_re - first_im * second_im, axis=(1, 2))
    trace_im = jnp.sum(first_re * second_im + first_im * second_re, axis=(1, 2))
    return jnp.stack([trace_re, trace_im], -1)


def run_blocks(step_fn, items, total):
    block = math.gcd(32, total)
    shaped = tuple((item.reshape((total // block, block) + item.shape[1:]) for item in items))
    result = lax.map(step_fn, shaped)
    return result.reshape((total,) + result.shape[2:])


def local(eigvecs, phase_index, perambulator, tile_sink, tile_sep, tile_diagram):
    tile_count = perambulator.shape[0]
    sinks = tile_sink[:, 0]
    cosine, sine = phases(phase_index)
    slices = lax.all_to_all(eigvecs, "space", split_axis=0, concat_axis=1, tiled=True)
    vecs = slices[0]
    right = make_right(vecs, cosine, sine)
    value = jnp.einsum("spck,spcol->okl", vecs, right, preferred_element_type=jnp.float32)
    elemental = value.astype(jnp.bfloat16)[None]
    gathered = lax.all_gather(elemental, "space", axis=0, tiled=True)
    time_count = gathered.shape[0]
    sources = jnp.mod(sinks - tile_sep, time_count)

    def holder_block(items):
        tiles, sink_ids, source_ids, diagram = items
        return contract_tiles(gathered[sink_ids], gathered[source_ids], tiles, diagram)

    correlator = run_blocks(holder_block, (perambulator, sinks, sources, tile_diagram), tile_count)
    return (elemental, correlator)


def solution(mesh):
    return jax.shard_map(
        local,
        mesh=mesh,
        in_specs=(
            P("groups", "space", None, None, None),
            P("groups"),
            P(("groups", "space"), None, None, None),
            P(("groups", "space"), None),
            P(("groups", "space")),
            P(("groups", "space")),
        ),
        out_specs=(P(("groups", "space"), None, None, None), P(("groups", "space"), None)),
        check_vma=False,
    )
```

profile of v0, /device:TPU:0, one launch (start us, length us, event | category | flops | bytes accessed | tf_op | source)
XLA Modules:
  0.0 76.8 jit_solution(16801960626893713510)
XLA Ops:
  7.2 0.0 copy-start.2
  7.2 0.0 copy-start
  7.2 7.6 %all-to-all-start = ((bf16[16,4,2,3,128]{4,2,3,1,0:T(2,128)(2,1)}), bf16[16,4,2,3,128]{4,2,3,1,0:T(2,128)(2,1)S(1)}, u32[]{:S(2)}, u32[]{:S(2)}) async-start(bf16[16,4,2,3,128]{4,2,3,1,0:T(2,128)(2,1)} %param.6), calls=%async_computation | async-start | bytes 196608 | tf_op jit(solution)/shard_map/all_to_all | solution.py:65
  14.7 0.0 all-gather.3.cloned.1.call-start
  14.9 7.3 %all-to-all-done = bf16[16,4,2,3,128]{4,2,3,1,0:T(2,128)(2,1)S(1)} async-done(((bf16[16,4,2,3,128]{4,2,3,1,0:T(2,128)(2,1)}), bf16[16,4,2,3,128]{4,2,3,1,0:T(2,128)(2,1)S(1)}, u32[]{:S(2)}, u32[]{:S(2)}) %all-to-all-start) | async-done | bytes 98336 | tf_op jit(solution)/shard_map/all_to_all | solution.py:65
  22.2 0.1 fusion.15
  22.3 0.1 fusion.21
  22.4 0.3 fusion
  22.6 0.7 copy.37
  23.4 0.0 all-gather.3.cloned.1.call-update
  23.4 0.1 slice_bitcast_fusion.5
  23.5 0.3 copy.40
  23.8 0.0 copy-start.4
  23.8 0.3 copy.42
  24.1 0.4 copy-done.4
  24.5 0.6 copy-done.3
  25.1 0.0 copy-start.5
  25.2 0.6 copy-done.5
  25.8 0.7 copy.49
  26.5 32.4 %all-gather.3.cloned.1.call-done = bf16[32,128,128]{2,1,0:T(8,128)(2,1)} async-done(((bf16[2,128,128]{2,1,0:T(8,128)(2,1)}), bf16[32,128,128]{2,1,0:T(8,128)(2,1)}) %all-gather.3.cloned.1.call-update) | async-done | bytes 1048592 | tf_op jit(solution)/shard_map/all_gather | solution.py:70
  59.0 2.9 %gather_fusion.1 = bf16[16,2,128,128]{3,2,1,0:T(8,128)(2,1)} fusion(bf16[16,2,128,128]{3,2,1,0:T(8,128)(2,1)} %bitcast.124, s32[1024]{0:T(1024)S(1)} %pad_clamp_fusion), kind=kCustom, calls=%fused_computation.1 | custom fusion | bytes 2097216 | tf_op jit(solution)/shard_map/while/body/eval_jaxpr/gather | solution.py:76
  61.9 2.0 %gather_fusion = bf16[16,2,128,128]{3,2,1,0:T(8,128)(2,1)S(1)} fusion(bf16[16,2,128,128]{3,2,1,0:T(8,128)(2,1)} %bitcast.125, s32[1024]{0:T(1024)S(1)} %pad_clamp_fusion.1), kind=kCustom, calls=%fused_computation | custom fusion | bytes 2097216 | tf_op jit(solution)/shard_map/while/body/eval_jaxpr/gather | solution.py:76
  63.9 1.5 %fusion.5 = f32[16,128,128]{2,1,0:T(8,128)S(1)} fusion(bf16[16,2,128,128]{3,2,1,0:T(8,128)(2,1)} %gather_fusion.1, pred[16]{0:T(512)(128)(4,1)S(1)} %broadcast_compare_fusion, bf16[16,128,128]{1,2,0:T(8,128)(2,1)S(1)} %copy.42, bf16[16,2,128,128]{3,2,1,0:T(8,128)(2,1)S(1)} %copy-done), kind=kOutput, calls=%fused_computation.24 | convolution fusion | flops 67633152 | bytes 2621952 | tf_op jit(solution)/shard_map/while/body/eval_jaxpr/bij,bjk->bik/dot_general | solution.py:30
  65.4 0.4 fusion.3
  65.7 0.8 %copy-done.1 = bf16[16,2,128,128]{3,2,1,0:T(8,128)(2,1)S(1)} copy-done((bf16[16,2,128,128]{3,2,1,0:T(8,128)(2,1)S(1)}, bf16[16,2,128,128]{3,2,1,0:T(8,128)(2,1)}, u32[]{:S(2)}) %copy-start.1) | copy-done | bytes 1048600
  66.6 0.4 fusion.6
  67.0 0.4 fusion.4
  67.4 0.4 convolution_add_fusion
  67.8 0.4 convolution_subtract_fusion
  68.2 0.4 convolution_subtract_fusion.1
  68.6 0.7 subtract_reduce_fusion
  69.3 0.6 pad_maximum_fusion
  (12 shorter events, 0.1 us)
Async XLA Ops:
  7.2 7.6 %copy-start.2 = (s32[64]{0:T(128)S(1)}, s32[64]{0:T(128)}, u32[]{:S(2)}) copy-start(s32[64]{0:T(128)} %param.7) | copy-start | bytes 772
  7.2 16.3 %copy-start = (bf16[16,2,128,128]{3,2,1,0:T(8,128)(2,1)S(1)}, bf16[16,2,128,128]{3,2,1,0:T(8,128)(2,1)}, u32[]{:S(2)}) copy-start(bf16[16,2,128,128]{3,2,1,0:T(8,128)(2,1)} %param.8) | copy-start | bytes 3145732
  7.2 14.9 %all-to-all-start = ((bf16[16,4,2,3,128]{4,2,3,1,0:T(2,128)(2,1)}), bf16[16,4,2,3,128]{4,2,3,1,0:T(2,128)(2,1)S(1)}, u32[]{:S(2)}, u32[]{:S(2)}) async-start(bf16[16,4,2,3,128]{4,2,3,1,0:T(2,128)(2,1)} %param.6), calls=%async_computation | async-start | bytes 196608 | tf_op jit(solution)/shard_map/all_to_all | solution.py:65
  14.7 44.2 %all-gather.3.cloned.1.call-start = ((), (), s32[]{:S(2)}) async-start(), calls=%async_computation.1 | async-start | bytes 1114112 | tf_op jit(solution)/shard_map/all_gather | solution.py:70
  23.8 0.7 copy-start.4
  24.5 0.7 copy-start.3
  25.1 0.7 copy-start.5
  65.3 1.2 %copy-start.1 = (bf16[16,2,128,128]{3,2,1,0:T(8,128)(2,1)S(1)}, bf16[16,2,128,128]{3,2,1,0:T(8,128)(2,1)}, u32[]{:S(2)}) copy-start(bf16[16,2,128,128]{3,2,1,0:T(8,128)(2,1)} %gather_fusion.1) | copy-start | bytes 3145732
Sparse Core Ops, SparseCore 0:
  23.5 35.3 all-gather.2
where the time goes:
time: 77.1 us; the launch traced here: 76.8 us
  waiting for transfers between devices  39.7 us (51%)
  between operations  14.2 us (18%)
  local copies, waits for them, and re-layouts  9.55 us (12%)
  starting transfers between devices  7.6 us (10%)
  matrix products  4.81 us (6%)
  other arithmetic  0.85 us (1%)
    all_gather x1, waiting for transfers between devices, local(): gathered = lax.all_gather(elemental, 'space', axis=0, tiled=True)  32.4 us
    all_to_all x1, starting transfers between devices, local(): lax.all_to_all(eigvecs, 'space', split_axis=0, concat_axis=1, tiled=True)  7.56 us
    all_to_all x1, waiting for transfers between devices, local(): lax.all_to_all(eigvecs, 'space', split_axis=0, concat_axis=1, tiled=True)  7.27 us
    dot_general x8, matrix products, mult(): jnp.einsum('bij,bjk->bik', left, right, preferred_element_type=jnp.float32)  4.56 us
    unnamed x13, local copies, waits for them, and re-layouts  3.24 us
    gather x1, local copies, waits for them, and re-layouts, holder_block(): gathered[source_ids]  2.92 us
    gather x1, local copies, waits for them, and re-layouts, holder_block(): gathered[sink_ids]  1.97 us
  transfers between devices with their start and end apart: 2, of which 2 were waited for; matrix products, arithmetic and copies ran while one was open for 2% of the time, Pallas kernels for 0%

commit v1 on v0

--- a/solution.py
+++ b/solution.py
@@ -67,7 +67,9 @@
     right = make_right(vecs, cosine, sine)
     value = jnp.einsum("spck,spcol->okl", vecs, right, preferred_element_type=jnp.float32)
     elemental = value.astype(jnp.bfloat16)[None]
-    gathered = lax.all_gather(elemental, "space", axis=0, tiled=True)
+    gathered = jnp.concatenate(
+        lax.all_to_all(jnp.stack([elemental] * lax.axis_size("space")), "space", 0, 0), axis=0
+    )
     time_count = gathered.shape[0]
     sources = jnp.mod(sinks - tile_sep, time_count)
 

time: 77.1 us -> 55 us (0.71)
  the two profiles are of different devices: /device:TPU:0 before, /device:TPU:11 now
where the time goes in v1:
time: 55 us; the launch traced here: 54.6 us
  waiting for transfers between devices  25.7 us (47%)
  starting transfers between devices  12.2 us (22%)
  local copies, waits for them, and re-layouts  10.1 us (18%)
  matrix products  4.89 us (9%)
  other arithmetic  0.85 us (2%)
  between operations  0.83 us (2%)
    all_to_all x1, waiting for transfers between devices, local(): lax.all_to_all(jnp.stack([elemental] * lax.axis_size('space')), 'space',...  20.3 us
    all_to_all x1, starting transfers between devices, local(): lax.all_to_all(eigvecs, 'space', split_axis=0, concat_axis=1, tiled=True)  6.59 us
    all_to_all x1, starting transfers between devices, local(): lax.all_to_all(jnp.stack([elemental] * lax.axis_size('space')), 'space',...  5.62 us
    all_to_all x1, waiting for transfers between devices, local(): lax.all_to_all(eigvecs, 'space', split_axis=0, concat_axis=1, tiled=True)  5.4 us
    dot_general x8, matrix products, mult(): jnp.einsum('bij,bjk->bik', left, right, preferred_element_type=jnp.float32)  4.63 us
    unnamed x15, local copies, waits for them, and re-layouts  2.87 us
    gather x1, local copies, waits for them, and re-layouts, holder_block(): gathered[sink_ids]  1.7 us
    gather x1, local copies, waits for them, and re-layouts, holder_block(): gathered[source_ids]  1.65 us
  transfers between devices with their start and end apart: 2, of which 2 were waited for; matrix products, arithmetic and copies ran while one was open for 6% of the time, Pallas kernels for 0%

profile of v1, /device:TPU:11, one launch (start us, length us, event | category | flops | bytes accessed | tf_op | source)
XLA Modules:
  0.0 54.6 jit_solution(18197460929390654230)
XLA Ops:
  0.6 0.0 copy-start.3
  0.6 6.6 %all-to-all-start = ((bf16[16,4,2,3,128]{4,2,3,1,0:T(2,128)(2,1)}), bf16[16,4,2,3,128]{4,2,3,1,0:T(2,128)(2,1)S(1)}, u32[]{:S(2)}, u32[]{:S(2)}) async-start(bf16[16,4,2,3,128]{4,2,3,1,0:T(2,128)(2,1)} %param.6), calls=%async_computation | async-start | bytes 196608 | tf_op jit(solution)/shard_map/all_to_all | solution.py:65
  7.2 0.0 copy-done.3
  7.3 5.4 %all-to-all-done = bf16[16,4,2,3,128]{4,2,3,1,0:T(2,128)(2,1)S(1)} async-done(((bf16[16,4,2,3,128]{4,2,3,1,0:T(2,128)(2,1)}), bf16[16,4,2,3,128]{4,2,3,1,0:T(2,128)(2,1)S(1)}, u32[]{:S(2)}, u32[]{:S(2)}) %all-to-all-start) | async-done | bytes 98336 | tf_op jit(solution)/shard_map/all_to_all | solution.py:65
  12.7 0.1 fusion.15
  12.8 0.1 fusion.21
  12.9 0.3 fusion
  13.2 0.1 copy.37
  13.3 1.2 %stack.39 = bf16[16,1,2,128,128]{4,3,2,1,0:T(8,128)(2,1)} broadcast(bf16[2,128,128]{2,1,0:T(8,128)(2,1)S(1)} %copy.37), dimensions={2,3,4} | broadcast | bytes 1114112 | tf_op jit(solution)/shard_map/stack | solution.py:71
  14.6 5.6 %all-to-all-start.1 = ((bf16[16,1,2,128,128]{4,3,2,1,0:T(8,128)(2,1)}), bf16[16,1,2,128,128]{4,3,2,1,0:T(8,128)(2,1)S(1)}, u32[]{:S(2)}, u32[]{:S(2)}) async-start(bf16[16,1,2,128,128]{4,3,2,1,0:T(8,128)(2,1)} %stack.39), calls=%async_computation.1 | async-start | bytes 2097152 | tf_op jit(solution)/shard_map/all_to_all | solution.py:71
  20.2 0.9 %slice_bitcast_fusion.5 = (bf16[16,128,128]{2,1,0:T(8,128)(2,1)S(1)}, bf16[16,128,128]{2,1,0:T(8,128)(2,1)}) fusion(bf16[16,2,128,128]{3,2,1,0:T(8,128)(2,1)S(1)} %copy-done), kind=kLoop, calls=%fused_computation.21 | loop fusion | bytes 2097152 | tf_op jit(solution)/shard_map/while/body/eval_jaxpr/squeeze | solution.py:32
  21.1 0.3 copy.40
  21.4 0.0 copy-start.5
  21.4 1.3 %copy.42 = bf16[16,128,128]{1,2,0:T(8,128)(2,1)S(1)} copy(bf16[16,128,128]{2,1,0:T(8,128)(2,1)} %get-tuple-element.34) | data formatting | bytes 1048576 | tf_op jit(solution)/shard_map/while/body/eval_jaxpr/squeeze | solution.py:33
  22.8 0.0 copy-start.4
  22.8 0.6 %copy-done.4 = s32[16]{0:T(128)S(1)} copy-done((s32[16]{0:T(128)S(1)}, s32[16]{0:T(128)}, u32[]{:S(2)}) %copy-start.4) | copy-done | bytes 88
  23.4 0.0 copy-start.6
  23.5 0.6 %copy-done.6 = s32[16]{0:T(128)S(1)} copy-done((s32[16]{0:T(128)S(1)}, s32[16]{0:T(128)}, u32[]{:S(2)}) %copy-start.6) | copy-done | bytes 88
  24.1 0.7 %copy.49 = bf16[1,2,128,128]{3,2,1,0:T(8,128)(2,1)} copy(bf16[1,2,128,128]{2,3,1,0:T(8,128)(2,1)S(1)} %bitcast.130) | data formatting | bytes 131072
  24.8 20.3 %all-to-all-done.1 = bf16[16,1,2,128,128]{4,3,2,1,0:T(8,128)(2,1)S(1)} async-done(((bf16[16,1,2,128,128]{4,3,2,1,0:T(8,128)(2,1)}), bf16[16,1,2,128,128]{4,3,2,1,0:T(8,128)(2,1)S(1)}, u32[]{:S(2)}, u32[]{:S(2)}) %all-to-all-start.1) | async-done | bytes 1048608 | tf_op jit(solution)/shard_map/all_to_all | solution.py:71
  45.1 1.7 %gather_fusion.1 = bf16[16,2,128,128]{3,2,1,0:T(8,128)(2,1)} fusion(bf16[16,2,128,128]{3,2,1,0:T(8,128)(2,1)S(1)} %bitcast.124, s32[1024]{0:T(1024)S(1)} %pad_clamp_fusion), kind=kCustom, calls=%fused_computation.1 | custom fusion | bytes 2097216 | tf_op jit(solution)/shard_map/while/body/eval_jaxpr/gather | solution.py:78
  46.8 1.7 %gather_fusion = bf16[16,2,128,128]{3,2,1,0:T(8,128)(2,1)} fusion(bf16[16,2,128,128]{3,2,1,0:T(8,128)(2,1)S(1)} %bitcast.125, s32[1024]{0:T(1024)S(1)} %pad_clamp_fusion.1), kind=kCustom, calls=%fused_computation | custom fusion | bytes 2097216 | tf_op jit(solution)/shard_map/while/body/eval_jaxpr/gather | solution.py:78
  48.5 1.5 %fusion.5 = f32[16,128,128]{2,1,0:T(8,128)S(1)} fusion(bf16[16,2,128,128]{3,2,1,0:T(8,128)(2,1)} %gather_fusion.1, pred[16]{0:T(512)(128)(4,1)S(1)} %broadcast_compare_fusion, bf16[16,128,128]{1,2,0:T(8,128)(2,1)S(1)} %copy.42, bf16[16,2,128,128]{3,2,1,0:T(8,128)(2,1)S(1)} %copy-done), kind=kOutput, calls=%fused_computation.24 | convolution fusion | flops 67633152 | bytes 2621952 | tf_op jit(solution)/shard_map/while/body/eval_jaxpr/bij,bjk->bik/dot_general | solution.py:30
  50.1 0.4 fusion.3
  50.4 0.8 %copy-done.2 = bf16[16,2,128,128]{3,2,1,0:T(8,128)(2,1)S(1)} copy-done((bf16[16,2,128,128]{3,2,1,0:T(8,128)(2,1)S(1)}, bf16[16,2,128,128]{3,2,1,0:T(8,128)(2,1)}, u32[]{:S(2)}) %copy-start.2) | copy-done | bytes 1048600
  51.3 0.4 fusion.6
  51.7 0.4 fusion.4
  52.1 0.4 convolution_add_fusion
  52.5 0.4 convolution_subtract_fusion
  52.9 0.4 convolution_subtract_fusion.1
  53.3 0.7 %subtract_reduce_fusion = (f32[16]{0:T(128)S(1)}, f32[16]{0:T(128)S(1)}) fusion(f32[16,128,128]{2,1,0:T(8,128)S(1)} %convolution_add_fusion, f32[16,128,128]{2,1,0:T(8,128)S(1)} %convolution_subtract_fusion.1, f32[16,128,128]{2,1,0:T(8,128)S(1)} %convolution_subtract_fusion, f32[16,128,128]{2,1,0:T(8,128)S(1)} %fusion.3, ...), kind=kOutput, calls=%fused_computation.9 | convolution fusion | flops 69730272 | bytes 5767808 | tf_op jit(solution)/shard_map/while/body/eval_jaxpr/bij,bjk->bik/dot_general | solution.py:30
  54.0 0.6 %pad_maximum_fusion = f32[16,2]{0,1:T(2,128)} fusion(f32[16,1]{0,1:T(1,128)S(1)} %bitcast.132, f32[16,1]{0,1:T(1,128)S(1)} %bitcast.131), kind=kLoop, calls=%fused_computation.48 | loop fusion | flops 32 | bytes 256 | tf_op jit(solution)/shard_map/while/body/eval_jaxpr/stack | solution.py:51
  (14 shorter events, 0.1 us)
Async XLA Ops:
  0.6 6.6 %copy-start.3 = (s32[64]{0:T(128)S(1)}, s32[64]{0:T(128)}, u32[]{:S(2)}) copy-start(s32[64]{0:T(128)} %param.7) | copy-start | bytes 772
  0.6 12.0 %all-to-all-start = ((bf16[16,4,2,3,128]{4,2,3,1,0:T(2,128)(2,1)}), bf16[16,4,2,3,128]{4,2,3,1,0:T(2,128)(2,1)S(1)}, u32[]{:S(2)}, u32[]{:S(2)}) async-start(bf16[16,4,2,3,128]{4,2,3,1,0:T(2,128)(2,1)} %param.6), calls=%async_computation | async-start | bytes 196608 | tf_op jit(solution)/shard_map/all_to_all | solution.py:65
  14.6 5.6 %copy-start = (bf16[16,2,128,128]{3,2,1,0:T(8,128)(2,1)S(1)}, bf16[16,2,128,128]{3,2,1,0:T(8,128)(2,1)}, u32[]{:S(2)}) copy-start(bf16[16,2,128,128]{3,2,1,0:T(8,128)(2,1)} %param.8) | copy-start | bytes 3145732
  14.6 30.6 %all-to-all-start.1 = ((bf16[16,1,2,128,128]{4,3,2,1,0:T(8,128)(2,1)}), bf16[16,1,2,128,128]{4,3,2,1,0:T(8,128)(2,1)S(1)}, u32[]{:S(2)}, u32[]{:S(2)}) async-start(bf16[16,1,2,128,128]{4,3,2,1,0:T(8,128)(2,1)} %stack.39), calls=%async_computation.1 | async-start | bytes 2097152 | tf_op jit(solution)/shard_map/all_to_all | solution.py:71
  21.4 1.3 %copy-start.5 = (s32[16,1]{0,1:T(1,128)S(1)}, s32[16,1]{0,1:T(1,128)}, u32[]{:S(2)}) copy-start(s32[16,1]{0,1:T(1,128)} %param.9) | copy-start | bytes 196
  22.8 0.7 %copy-start.4 = (s32[16]{0:T(128)S(1)}, s32[16]{0:T(128)}, u32[]{:S(2)}) copy-start(s32[16]{0:T(128)} %param.10) | copy-start | bytes 196
  23.4 0.7 %copy-start.6 = (s32[16]{0:T(128)S(1)}, s32[16]{0:T(128)}, u32[]{:S(2)}) copy-start(s32[16]{0:T(128)} %param.11) | copy-start | bytes 196
  48.5 1.6 %copy-start.1 = (bf16[16,2,128,128]{3,2,1,0:T(8,128)(2,1)S(1)}, bf16[16,2,128,128]{3,2,1,0:T(8,128)(2,1)}, u32[]{:S(2)}) copy-start(bf16[16,2,128,128]{3,2,1,0:T(8,128)(2,1)} %gather_fusion) | copy-start | bytes 3145732
  50.0 1.2 %copy-start.2 = (bf16[16,2,128,128]{3,2,1,0:T(8,128)(2,1)S(1)}, bf16[16,2,128,128]{3,2,1,0:T(8,128)(2,1)}, u32[]{:S(2)}) copy-start(bf16[16,2,128,128]{3,2,1,0:T(8,128)(2,1)} %gather_fusion.1) | copy-start | bytes 3145732
